TPU v7x, 256 devices: a whole 4x4x8 slice. The times are simulated.
256 devices in a mesh: row: 32 (over z, y_lo, core), col: 8 (over y_hi, x).
Axes of the slice: x: 4, y: 4 (y_hi: 2, y_lo: 2; y = y_hi * 2 + y_lo), z: 8, core: 2. Of those that a mesh axis runs over, the one named last changes fastest.
Arguments:
- features: bfloat16 [32768, 128], P(('col', 'row')), may hold values from -96 to 96
- weight: bfloat16 [128, 256], replicated, may hold values from -0.5 to 0.5
- bias: float32 [256], replicated, may hold values from -3 to 3
- cotangent: bfloat16 [32768, 256], P(('row', 'col')), may hold values from -6 to 6
- tile_values: bfloat16 [32, 8, 256, 128, 128], P('row', 'col'), may hold values from 0 to 4, as said below
- tile_pos: int32 [32, 8, 2, 256], P('row', 'col'), may hold values from 0 to 31, as said below
- tile_count: int32 [32, 8], P('row', 'col'), may hold values from 0 to 256, as said below
- block_perm: int32 [256], replicated, may hold values from 0 to 255, as said below
Outputs:
- hidden: bfloat16 [32768, 256], P(('row', 'col'))
- weight_grad: float32 [128, 256], replicated
- bias_grad: float32 [256], replicated
Inputs may be any that keep to these rules, and one draw needn't show every extreme that they name: `tile_values`: entries are 0 or a weight of at least 0.25; slots t at or beyond tile_count[r, c] belong to no tile. `tile_pos`: entry [r, c, 0, t] is the slot's tile row, below 8, within row block r, and [r, c, 1, t] its tile column, below 32, within column block c, both in the reordered numbering; the slots of one cell hold distinct positions. `tile_count`: every draw has a cell with 256 live slots. `block_perm`: each aligned run of 8 entries is a permutation of that run's own indices.
All inputs are finite; a program needn't handle non-finite values.
Results may differ from a plain program's by a relative error of at most 0.0059.
Values may be sent and summed in bfloat16 or wider, within the bound.
No kernel may reach another device: no remote copies, remote signals or barrier semaphores. Data moves between devices by JAX's collectives and lax.ppermute only.
A program may use at most 64 MiB of HBM per device.

v0:
```python
import jax
import jax.numpy as jnp
from jax import lax
from jax.sharding import PartitionSpec as P


def local_index(block_perm, tile_axis, block_index, run_length):
    return jnp.take(block_perm, block_index * run_length + tile_axis) - block_index * run_length


def body(features, weight, bias, cotangent, tile_values, tile_pos, tile_count, block_perm):
    row_count = lax.axis_size("row")
    col_count = lax.axis_size("col")
    row_index = lax.axis_index("row")
    col_index = lax.axis_index("col")
    packed = tile_values[0, 0]
    positions = tile_pos[0, 0]
    live_count = tile_count[0, 0]
    max_tiles = packed.shape[0]
    tile_size = packed.shape[1]
    feat_width = features.shape[1]
    row_tiles = block_perm.shape[0] // row_count
    col_tiles = row_tiles * row_count // col_count
    block_tiles = min(64, max_tiles)
    lane_index = jnp.arange(block_tiles, dtype=jnp.int32)
    own_rows = local_index(block_perm, positions[0], row_index, row_tiles)
    own_cols = local_index(block_perm, positions[1], col_index, col_tiles)

    def degree_step(block_step, totals):
        row_acc, col_acc = totals
        slot_number = block_step * block_tiles + lane_index
        is_live = slot_number < live_count
        clamped = jnp.minimum(slot_number, max_tiles - 1)
        values = jnp.take(packed, clamped, axis=0).astype(jnp.float32)
        row_part = jnp.sum(values, axis=2)
        col_part = jnp.sum(values, axis=1)
        row_part = jnp.where(is_live[:, None], row_part, 0.0)
        col_part = jnp.where(is_live[:, None], col_part, 0.0)
        row_acc = row_acc.at[jnp.take(own_rows, clamped)].add(row_part)
        col_acc = col_acc.at[jnp.take(own_cols, clamped)].add(col_part)
        return (row_acc, col_acc)

    degree_blocks = (live_count + block_tiles - 1) // block_tiles
    row_acc, col_acc = lax.fori_loop(
        jnp.int32(0),
        degree_blocks,
        degree_step,
        (
            jnp.zeros((row_tiles, tile_size), jnp.float32),
            jnp.zeros((col_tiles, tile_size), jnp.float32),
        ),
    )
    col_part_flat = col_acc.reshape(col_tiles * tile_size)
    col_share = lax.psum_scatter(col_part_flat, "row", scatter_dimension=0, tiled=True)
    scaled = (lax.rsqrt(1.0 + col_share)[:, None] * features.astype(jnp.float32)).astype(
        jnp.bfloat16
    )
    gathered = lax.all_gather(scaled, "row", axis=0, tiled=True)
    feature_tiles = gathered.reshape(col_tiles, tile_size, feat_width)
    list_length = packed.shape[0]

    def product_step(block_step, partial_value):
        logical = block_step * block_tiles + lane_index
        is_live = logical < live_count
        is_upper = logical >= live_count
        source = jnp.where(is_upper, logical - live_count, logical)
        source = jnp.clip(source, 0, list_length - 1)
        slot_number = jnp.minimum(is_upper.astype(jnp.int32), 1 - 1)
        tile_block = jnp.take(packed, source, axis=0)
        tile_block = jnp.where(is_live[:, None, None], tile_block, jnp.zeros((), jnp.bfloat16))
        inputs = jnp.take(feature_tiles, jnp.take(own_cols, source), axis=0)
        products = jnp.einsum(
            "bpq,bqf->bpf", tile_block, inputs, preferred_element_type=jnp.float32
        )
        return partial_value.at[slot_number, jnp.take(own_rows, source)].add(products)

    product_blocks = (live_count + block_tiles - 1) // block_tiles
    initial = jnp.zeros((1, row_tiles, tile_size, feat_width), jnp.float32)
    partial_value = lax.fori_loop(jnp.int32(0), product_blocks, product_step, initial)
    own_sum = partial_value[0]
    row_part_flat = row_acc.reshape(row_tiles * tile_size)
    summed, degree_share = (
        lax.psum_scatter(
            own_sum.reshape(row_tiles * tile_size, feat_width),
            "col",
            scatter_dimension=0,
            tiled=True,
        ),
        lax.psum_scatter(row_part_flat, "col", scatter_dimension=0, tiled=True),
    )
    aggregated = (lax.rsqrt(1.0 + degree_share)[:, None] * summed).astype(jnp.bfloat16)
    preact = jnp.dot(aggregated, weight, preferred_element_type=jnp.float32) + bias
    logistic = jax.nn.sigmoid(preact)
    hidden = (preact * logistic).astype(jnp.bfloat16)
    preact_grad = (
        cotangent.astype(jnp.float32) * logistic * (1.0 + preact * (1.0 - logistic))
    ).astype(jnp.bfloat16)
    weight_part = jnp.einsum(
        "nf,nh->fh", aggregated, preact_grad, preferred_element_type=jnp.float32
    )
    bias_part = jnp.sum(preact_grad.astype(jnp.float32), axis=0)
    weight_sum, bias_sum = lax.psum((weight_part, bias_part), ("row", "col"))
    inverse_root = lax.rsqrt(jnp.float32(summed.shape[0] * row_count * col_count))
    return (hidden, weight_sum * inverse_root, bias_sum * inverse_root)


def solution(mesh):
    placed = (
        P(("col", "row"), None),
        P(),
        P(),
        P(("row", "col"), None),
        P("row", "col", None, None, None),
        P("row", "col", None, None),
        P("row", "col"),
        P(),
    )
    return jax.shard_map(
        body,
        mesh=mesh,
        in_specs=placed,
        out_specs=(P(("row", "col"), None), P(), P()),
        check_vma=False,
    )
```

profile of v0, /device:TPU:2, one launch (start us, length us, event | category | flops | bytes accessed | tf_op | source)
XLA Modules:
  0.0 723.7 jit_solution(14614431443404107920)
XLA Ops:
  8.7 2.0 gather_fusion.8
  10.7 2.0 gather_fusion.7
  12.7 9.5 %while.24 = (s32[]{:T(128)}, f32[8,128]{1,0:T(8,128)S(1)}, f32[32,128]{1,0:T(8,128)S(1)}, s32[]{:T(128)}, s32[256]{0:T(256)S(1)}, /*index=5*/s32[]{:T(128)}, bf1...) while((s32[]{:T(128)}, f32[8,128]{1,0:T(8,128)S(1)}, ...), condition=%wide.region_5.9_spmd.clone, body=%wide.region_0.8_spmd.clone.sunk | while | flops 4213635 | bytes 6451793 | solution.py:44
  13.4 0.8 gather_fusion.1
  14.2 0.8 gather_fusion
  15.0 4.3 gather_fusion.2
  19.4 0.9 convert_reduce_fusion.4
  20.2 1.0 scatter_custom_fusion.15
  21.2 1.0 scatter_custom_fusion.16
  22.2 122.7 %all-reduce.1 = f32[4096]{0:T(1024)S(1)} all-reduce(f32[4096]{0:T(1024)S(1)} %bitcast.44), channel_id=3, replica_groups=mesh['row'=32,'col'=8] {'row'}, use_global_device_ids=true, to_apply=%region_7.11.clone | all-reduce | flops 4096 | bytes 32768
  147.1 74.5 %all-gather.2.cloned.1.call-done = bf16[4096,128]{1,0:T(8,128)(2,1)} async-done(((bf16[128,128]{1,0:T(8,128)(2,1)}), bf16[4096,128]{1,0:T(8,128)(2,1)}) %all-gather.2.cloned.1.call-update) | async-done | bytes 1048592 | tf_op jit(solution)/shard_map/all_gather | solution.py:58
  221.6 24.0 %while.25 = (s32[]{:T(128)}, f32[1,8,128,128]{3,2,1,0:T(8,128)S(1)}, s32[]{:T(128)}, s32[]{:T(128)}, s32[256]{0:T(256)S(1)}, /*index=5*/bf16[256,128,128]{2,1,0:...) while((s32[]{:T(128)}, f32[1,8,128,128]{3,2,1,0:T(8,128)S(1)}, ...), condition=%wide.region_10.14_spmd.clone, body=%wide.region_8.13_spmd.clone.sunk | while | flops 272634240 | bytes 41956408 | solution.py:79
  223.2 0.8 gather_fusion.3
  224.7 2.2 gather_fusion.6
  226.8 5.7 gather_fusion.4
  232.5 4.3 fusion.45
  236.8 8.8 %scatter_fusion = f32[8,128,128]{2,1,0:T(8,128)S(1)} fusion(f32[8,128,128]{2,1,0:T(8,128)S(1)} %bitcast.39, s32[64]{0:T(128)S(1)} %fusion.44, f32[64,128,128]{2,1,0:T(8,128)} %fusion.45), kind=kCustom, calls=%fused_computation.11.clone.clone.1 | custom fusion | flops 1048576 | bytes 12583168 | tf_op jit(solution)/shard_map/while/body/scatter-add | solution.py:75
  247.7 43.6 %all-reduce = f32[1024]{0:T(1024)S(1)} all-reduce(f32[1024]{0:T(1024)S(1)} %bitcast.45), channel_id=2, replica_groups=mesh['row'=32,'col'=8] {'col'}, use_global_device_ids=true, to_apply=%region_6.10.clone | all-reduce | flops 1024 | bytes 8192
  291.4 102.7 %reduce-scatter.2.cloned.1.call-done = f32[128,128]{1,0:T(8,128)} async-done(((f32[1024,128]{1,0:T(8,128)}), f32[128,128]{1,0:T(8,128)}) %reduce-scatter.2.cloned.1.call-update) | async-done | bytes 65552 | tf_op jit(solution)/shard_map/reduce_scatter | solution.py:83
  394.1 1.7 convert_reduce_fusion.2
  395.8 73.9 %psum.15 = f32[256]{0:T(256)S(1)} all-reduce(f32[256]{0:T(256)S(1)} %get-tuple-element.182), channel_id=1, replica_groups=mesh['row'=32,'col'=8] {'row','col'}, use_global_device_ids=true, to_apply=%region_14.18 | all-reduce | flops 256 | bytes 2048 | tf_op jit(solution)/shard_map/psum | solution.py:102
  469.8 1.8 fusion.33
  472.1 243.5 %all-reduce.4.cloned.1.call-done = f32[128,256]{1,0:T(8,128)} async-done(((f32[128,256]{1,0:T(8,128)}), f32[128,256]{1,0:T(8,128)}) %all-reduce.4.cloned.1.call-update) | async-done | bytes 131088 | tf_op jit(solution)/shard_map/psum | solution.py:102
  715.6 1.6 broadcast_multiply_fusion
  (49 shorter events, 7.3 us)
Async XLA Ops:
  7.2 386.9 %copy-start = (bf16[128,256]{1,0:T(8,128)(2,1)S(1)}, bf16[128,256]{1,0:T(8,128)(2,1)}, u32[]{:S(2)}) copy-start(bf16[128,256]{1,0:T(8,128)(2,1)} %param.19) | copy-start | bytes 196612
  7.2 214.3 %all-gather.2.cloned.1.call-start = ((), (), s32[]{:S(2)}) async-start(), calls=%async_computation.1 | async-start | bytes 1081344 | tf_op jit(solution)/shard_map/all_gather | solution.py:58
  12.7 132.3 %copy-start.8 = (u32[256]{0:T(256)S(1)}, u32[256]{0:T(256)}, u32[]{:S(2)}) copy-start(u32[256]{0:T(256)} %constant.133) | copy-start | bytes 3076
  12.7 133.6 %copy-start.4 = (bf16[128,128]{1,0:T(8,128)(2,1)S(1)}, bf16[128,128]{1,0:T(8,128)(2,1)}, u32[]{:S(2)}) copy-start(bf16[128,128]{1,0:T(8,128)(2,1)} %param.18) | copy-start | bytes 98308
  12.7 381.4 %copy-start.5 = (bf16[128,256]{1,0:T(8,128)(2,1)S(1)}, bf16[128,256]{1,0:T(8,128)(2,1)}, u32[]{:S(2)}) copy-start(bf16[128,256]{1,0:T(8,128)(2,1)} %param.21) | copy-start | bytes 196612
  147.0 247.1 %reduce-scatter.2.cloned.1.call-start = ((), (), s32[]{:S(2)}) async-start(), calls=%async_computation.2 | async-start | bytes 589824 | tf_op jit(solution)/shard_map/reduce_scatter | solution.py:83
  221.6 24.9 %copy-start.7 = (u32[256]{0:T(256)S(1)}, u32[256]{0:T(256)}, u32[]{:S(2)}) copy-start(u32[256]{0:T(256)} %constant.129) | copy-start | bytes 3076
  221.6 172.5 %copy-start.6 = (f32[256]{0:T(256)S(1)}, f32[256]{0:T(256)}, u32[]{:S(2)}) copy-start(f32[256]{0:T(256)} %param.20) | copy-start | bytes 3076
  221.6 3.1 copy-start.2
  226.8 5.7 copy-start.3
  245.6 0.8 copy-start.1
  246.4 469.2 %all-reduce.4.cloned.1.call-start = ((), (), s32[]{:S(2)}) async-start(), calls=%async_computation.3 | async-start | bytes 262144 | tf_op jit(solution)/shard_map/psum | solution.py:102
Sparse Core Ops, SparseCore 0:
  147.1 74.3 all-gather.1
  246.6 147.4 reduce-scatter.1
  471.7 243.8 all-reduce.3
where the time goes:
time: 725 us; the launch traced here: 724 us
  waiting for transfers between devices  421 us (58%)
  blocking collectives  240 us (33%)
  local copies, waits for them, and re-layouts  21.3 us (3%)
  other arithmetic  17.5 us (2%)
  between operations  15.9 us (2%)
  matrix products  7.81 us (1%)
    psum x1, waiting for transfers between devices, body(): weight_sum, bias_sum = lax.psum((weight_part, bias_part), ('row', 'col'))  243 us
    unnamed x2, blocking collectives  166 us
    reduce_scatter x1, waiting for transfers between devices, body(): lax.psum_scatter(own_sum.reshape(row_tiles * tile_size, feat_width), 'col...  103 us
    all_gather x1, waiting for transfers between devices, body(): gathered = lax.all_gather(scaled, 'row', axis=0, tiled=True)  74.5 us
    psum x1, blocking collectives, body(): weight_sum, bias_sum = lax.psum((weight_part, bias_part), ('row', 'col'))  73.9 us
  transfers between devices with their start and end apart: 3, of which 3 were waited for; matrix products, arithmetic and copies ran while one was open for 0% of the time, Pallas kernels for 0%

commit v1 on v0

--- a/solution.py
+++ b/solution.py
@@ -55,7 +55,10 @@
     scaled = (lax.rsqrt(1.0 + col_share)[:, None] * features.astype(jnp.float32)).astype(
         jnp.bfloat16
     )
-    gathered = lax.all_gather(scaled, "row", axis=0, tiled=True)
+    size = lax.axis_size("row")
+    blocks = jnp.stack([scaled for _ in range(size)])
+    blocks = lax.all_to_all(blocks, "row", split_axis=0, concat_axis=0)
+    gathered = jnp.concatenate(blocks, axis=0)
     feature_tiles = gathered.reshape(col_tiles, tile_size, feat_width)
     list_length = packed.shape[0]
 

time: 725 us -> 695 us (0.959)
  waiting for transfers between devices: 421 us -> 345 us
  blocking collectives: 240 us -> 285 us
    all_gather x1 -> x0, waiting for transfers between devices: 74.5 us -> none  [body(): gathered = lax.all_gather(scaled, 'row', axis=0, tiled=True)]
    all_to_all x0 -> x1, blocking collectives: none -> 47.1 us  [body(): blocks = lax.all_to_all(blocks, 'row', split_axis=0, concat_axis=0)]
  transfers between devices with their start and end apart: 3 -> 2, of which waited for: 3 -> 2; matrix products, arithmetic and copies ran while one was open for 0% -> 0% of each run, Pallas kernels for 0% -> 0%
where the time goes in v1:
time: 695 us; the launch traced here: 693 us
  waiting for transfers between devices  345 us (50%)
  blocking collectives  285 us (41%)
  local copies, waits for them, and re-layouts  21.4 us (3%)
  other arithmetic  16.8 us (2%)
  between operations  16.2 us (2%)
  matrix products  8.42 us (1%)
    psum x1, waiting for transfers between devices, body(): weight_sum, bias_sum = lax.psum((weight_part, bias_part), ('row', 'col'))  244 us
    unnamed x2, blocking collectives  164 us
    reduce_scatter x1, waiting for transfers between devices, body(): lax.psum_scatter(own_sum.reshape(row_tiles * tile_size, feat_width), 'col...  102 us
    psum x1, blocking collectives, body(): weight_sum, bias_sum = lax.psum((weight_part, bias_part), ('row', 'col'))  73.9 us
    all_to_all x1, blocking collectives, body(): blocks = lax.all_to_all(blocks, 'row', split_axis=0, concat_axis=0)  47.1 us
  transfers between devices with their start and end apart: 2, of which 2 were waited for; matrix products, arithmetic and copies ran while one was open for 0% of the time, Pallas kernels for 0%

profile of v1, /device:TPU:2, one launch (start us, length us, event | category | flops | bytes accessed | tf_op | source)
XLA Modules:
  0.0 693.4 jit_solution(3747786525189773888)
XLA Ops:
  8.7 2.0 gather_fusion.8
  10.7 2.0 gather_fusion.7
  12.7 9.5 %while.24 = (s32[]{:T(128)}, f32[8,128]{1,0:T(8,128)S(1)}, f32[32,128]{1,0:T(8,128)S(1)}, s32[]{:T(128)}, s32[256]{0:T(256)S(1)}, /*index=5*/s32[]{:T(128)}, bf1...) while((s32[]{:T(128)}, f32[8,128]{1,0:T(8,128)S(1)}, ...), condition=%wide.region_5.9_spmd.clone, body=%wide.region_0.8_spmd.clone.sunk | while | flops 4213635 | bytes 6451793 | solution.py:44
  13.4 0.8 gather_fusion.1
  14.2 0.8 gather_fusion
  15.0 4.3 gather_fusion.2
  19.4 0.9 convert_reduce_fusion.4
  20.2 1.0 scatter_custom_fusion.15
  21.2 1.0 scatter_custom_fusion.16
  22.2 122.7 %all-reduce.1 = f32[4096]{0:T(1024)S(1)} all-reduce(f32[4096]{0:T(1024)S(1)} %bitcast.42), channel_id=3, replica_groups=mesh['row'=32,'col'=8] {'row'}, use_global_device_ids=true, to_apply=%region_7.11.clone | all-reduce | flops 4096 | bytes 32768
  146.6 47.1 %all_to_all.5 = bf16[32,128,128]{2,1,0:T(8,128)(2,1)S(1)} all-to-all(bf16[32,128,128]{2,1,0:T(8,128)(2,1)S(1)} %stack.2), channel_id=1, replica_groups=mesh['row'=32,'col'=8] {'row'}, dimensions={0} | all-to-all | bytes 2097152 | tf_op jit(solution)/shard_map/all_to_all | solution.py:60
  193.8 24.4 %while.25 = (s32[]{:T(128)}, f32[1,8,128,128]{3,2,1,0:T(8,128)S(1)}, s32[]{:T(128)}, s32[]{:T(128)}, s32[256]{0:T(256)S(1)}, /*index=5*/bf16[256,128,128]{2,1,0:...) while((s32[]{:T(128)}, ...), condition=%wide.region_10.14_spmd.clone, body=%wide.region_8.13_spmd.clone.sunk | while | flops 272634240 | bytes 29373440 | solution.py:82
  195.3 0.8 gather_fusion.3
  196.8 2.2 gather_fusion.6
  199.0 5.5 gather_fusion.4
  204.5 4.9 fusion.45
  209.4 8.8 %scatter_fusion = f32[8,128,128]{2,1,0:T(8,128)S(1)} fusion(f32[8,128,128]{2,1,0:T(8,128)S(1)} %bitcast.38, s32[64]{0:T(128)S(1)} %fusion.44, f32[64,128,128]{2,1,0:T(8,128)} %fusion.45), kind=kCustom, calls=%fused_computation.11.clone.clone.1 | custom fusion | flops 1048576 | bytes 12583168 | tf_op jit(solution)/shard_map/while/body/scatter-add | solution.py:78
  220.3 41.4 %all-reduce = f32[1024]{0:T(1024)S(1)} all-reduce(f32[1024]{0:T(1024)S(1)} %bitcast.43), channel_id=2, replica_groups=mesh['row'=32,'col'=8] {'col'}, use_global_device_ids=true, to_apply=%region_6.10.clone | all-reduce | flops 1024 | bytes 8192
  261.8 101.6 %reduce-scatter.2.cloned.1.call-done = f32[128,128]{1,0:T(8,128)} async-done(((f32[1024,128]{1,0:T(8,128)}), f32[128,128]{1,0:T(8,128)}) %reduce-scatter.2.cloned.1.call-update) | async-done | bytes 65552 | tf_op jit(solution)/shard_map/reduce_scatter | solution.py:86
  363.4 1.7 convert_reduce_fusion.2
  365.2 73.9 %psum.15 = f32[256]{0:T(256)S(1)} all-reduce(f32[256]{0:T(256)S(1)} %get-tuple-element.182), channel_id=1, replica_groups=mesh['row'=32,'col'=8] {'row','col'}, use_global_device_ids=true, to_apply=%region_14.18 | all-reduce | flops 256 | bytes 2048 | tf_op jit(solution)/shard_map/psum | solution.py:105
  439.1 1.8 fusion.33
  441.4 243.6 %all-reduce.4.cloned.1.call-done = f32[128,256]{1,0:T(8,128)} async-done(((f32[128,256]{1,0:T(8,128)}), f32[128,256]{1,0:T(8,128)}) %all-reduce.4.cloned.1.call-update) | async-done | bytes 131088 | tf_op jit(solution)/shard_map/psum | solution.py:105
  685.0 1.6 broadcast_multiply_fusion
  (44 shorter events, 6.8 us)
Async XLA Ops:
  7.2 356.3 %copy-start = (bf16[128,256]{1,0:T(8,128)(2,1)S(1)}, bf16[128,256]{1,0:T(8,128)(2,1)}, u32[]{:S(2)}) copy-start(bf16[128,256]{1,0:T(8,128)(2,1)} %param.19) | copy-start | bytes 196612
  7.2 356.2 %reduce-scatter.2.cloned.1.call-start = ((), (), s32[]{:S(2)}) async-start(), calls=%async_computation.2 | async-start | bytes 589824 | tf_op jit(solution)/shard_map/reduce_scatter | solution.py:86
  12.7 132.2 %copy-start.6 = (u32[256]{0:T(256)S(1)}, u32[256]{0:T(256)}, u32[]{:S(2)}) copy-start(u32[256]{0:T(256)} %constant.133) | copy-start | bytes 3076
  12.7 133.6 %copy-start.2 = (bf16[128,128]{1,0:T(8,128)(2,1)S(1)}, bf16[128,128]{1,0:T(8,128)(2,1)}, u32[]{:S(2)}) copy-start(bf16[128,128]{1,0:T(8,128)(2,1)} %param.18) | copy-start | bytes 98308
  193.8 25.3 %copy-start.5 = (u32[256]{0:T(256)S(1)}, u32[256]{0:T(256)}, u32[]{:S(2)}) copy-start(u32[256]{0:T(256)} %constant.129) | copy-start | bytes 3076
  193.8 169.6 %copy-start.3 = (bf16[128,256]{1,0:T(8,128)(2,1)S(1)}, bf16[128,256]{1,0:T(8,128)(2,1)}, u32[]{:S(2)}) copy-start(bf16[128,256]{1,0:T(8,128)(2,1)} %param.21) | copy-start | bytes 196612
  193.8 169.6 %copy-start.4 = (f32[256]{0:T(256)S(1)}, f32[256]{0:T(256)}, u32[]{:S(2)}) copy-start(f32[256]{0:T(256)} %param.20) | copy-start | bytes 3076
  218.2 0.8 copy-start.1
  219.0 466.0 %all-reduce.4.cloned.1.call-start = ((), (), s32[]{:S(2)}) async-start(), calls=%async_computation.3 | async-start | bytes 262144 | tf_op jit(solution)/shard_map/psum | solution.py:105
Sparse Core Ops, SparseCore 0:
  219.1 144.2 reduce-scatter.1
  441.0 243.9 all-reduce.3
